TPU v7x, 32 devices: a whole 2x2x4 slice. The times are simulated.
32 devices in a mesh: seq: 8 (over y, x, core), dp: 4 (over z).
Axes of the slice: x: 2, y: 2, z: 4, core: 2. Of those that a mesh axis runs over, the one named last changes fastest.
Arguments:
- history: bfloat16 [9, 1024, 4096], P(None, 'seq', 'dp'), may hold values from -6 to 6
- cotangent: bfloat16 [1024, 4096], P('seq', 'dp'), may hold values from -6 to 6
- bucket_len: int32 [4, 8, 2], P('dp', 'seq'), may hold values from 32 to 96, as said below
- valid_len: int32 [4, 8, 2], P('dp', 'seq'), may hold values from 1 to 96, as said below
- gen_gain: float32 [1024], replicated, may hold values from 0.25 to 1.75
- gen_in: bfloat16 [1024, 40], replicated, may hold values from -0.1875 to 0.1875
- gen_out: float32 [40, 4, 9], replicated, may hold values from -1 to 1
- gen_bias: float32 [4, 9], replicated, may hold values from -3 to 3
- norm_gain: float32 [2, 1024], replicated, may hold values from 0.25 to 1.75
- norm_bias: float32 [2, 1024], replicated, may hold values from -2 to 2
- w_in: bfloat16 [1024, 7, 1024], P('seq'), may hold values from -0.1875 to 0.1875
- in_bias: float32 [7, 1024], replicated, may hold values from -2 to 2
- w_out: bfloat16 [1024, 1024], P('seq'), may hold values from -0.75 to 0.75
- w_down: bfloat16 [1024, 4096], P('seq'), may hold values from -0.09375 to 0.09375
- out_bias: float32 [1024], replicated, may hold values from -2 to 2
Outputs:
- new_state: bfloat16 [1024, 4096], P('seq', 'dp')
- history_grad: bfloat16 [9, 1024, 4096], P(None, 'seq', 'dp')
- mix_mean: float32 [4, 9], replicated
- mix_var: float32 [4, 9], replicated
- gen_gain_grad: float32 [1024], replicated
- gen_in_grad: float32 [1024, 40], replicated
- gen_out_grad: float32 [40, 4, 9], replicated
- gen_bias_grad: float32 [4, 9], replicated
- norm_gain_grad: float32 [2, 1024], replicated
- norm_bias_grad: float32 [2, 1024], replicated
- w_in_grad: float32 [1024, 7, 1024], P('seq')
- in_bias_grad: float32 [7, 1024], replicated
- w_out_grad: float32 [1024, 1024], P('seq')
- w_down_grad: float32 [1024, 4096], P('seq')
- out_bias_grad: float32 [1024], replicated
Inputs may be any that keep to these rules, and one draw needn't show every extreme that they name: `bucket_len`: the two buckets of one token block together hold 128 tokens. Each bucket's valid tokens are its first valid_len tokens, at least one and at most the bucket's length.
All inputs are finite; a program needn't handle non-finite values.
Results may differ from a plain program's by a relative error of at most 0.015.
Values may be sent and summed in bfloat16 or wider, within the bound.
A program may use at most 256 MiB of HBM per device.

v0:
```python
import math
import jax
import jax.numpy as jnp
from jax import lax
from jax.sharding import PartitionSpec as P

HEADS = 16
HEAD_DIM = 64
ROT = 16
ln_eps = 1e-05
rms_eps = 1e-06
masked_score = -1e30
highest = lax.Precision.HIGHEST


def gelu_exact(values):
    return jax.nn.gelu(values, approximate=False)


def rotary_tables(position):
    freq_index = jnp.arange(ROT // 2, dtype=jnp.float32)
    inverse_freq = jnp.exp(freq_index * (-2.0 * math.log(10000.0) / ROT))
    angles = position.astype(jnp.float32)[:, None] * inverse_freq[None, :]
    return (jnp.cos(angles), jnp.sin(angles))


def rotate(values, cosine, sine):
    half = ROT // 2
    former = values[..., :half]
    latter = values[..., half:ROT]
    cos_heads = cosine[:, None, :]
    sin_heads = sine[:, None, :]
    return jnp.concatenate(
        [
            former * cos_heads - latter * sin_heads,
            latter * cos_heads + former * sin_heads,
            values[..., ROT:],
        ],
        axis=-1,
    )


def token_layout(lengths, counts, tokens):
    index = jnp.arange(tokens, dtype=jnp.int32)
    second = index >= lengths[0]
    position = index - jnp.where(second, lengths[0], 0)
    valid = position < jnp.where(second, counts[1], counts[0])
    return (second, position, valid)


def normalize(streams):
    centre = jnp.mean(streams, axis=-1, keepdims=True)
    centred = streams - centre
    inverse = lax.rsqrt(jnp.mean(centred * centred, axis=-1, keepdims=True) + ln_eps)
    return (centred * inverse, inverse)


def normalize_back(grad_scaled, scaled, inverse):
    mean_grad = jnp.mean(grad_scaled, axis=-1, keepdims=True)
    mean_along = jnp.mean(grad_scaled * scaled, axis=-1, keepdims=True)
    return inverse * (grad_scaled - mean_grad - scaled * mean_along)


def per_device(
    history,
    cotangent,
    bucket_len,
    valid_len,
    gen_gain,
    gen_in,
    gen_out,
    gen_bias,
    norm_gain,
    norm_bias,
    w_in,
    in_bias,
    w_out,
    w_down,
    out_bias,
):
    states = history.shape[0]
    stacked = jnp.concatenate([history, cotangent[None]], axis=0)
    arrived = lax.all_to_all(stacked, "seq", split_axis=2, concat_axis=1, tiled=True)
    arrived_rows = jnp.swapaxes(arrived, 1, 2)
    hist_local = arrived_rows[:states]
    cot_local = arrived_rows[states]
    tokens = hist_local.shape[1]
    width = hist_local.shape[2]
    second, position, valid = token_layout(bucket_len.reshape(2), valid_len.reshape(2), tokens)
    valid_float = valid.astype(jnp.float32)
    last = hist_local[states - 1].astype(jnp.float32)
    rms = lax.rsqrt(jnp.mean(last * last, axis=-1, keepdims=True) + rms_eps)
    gen_normed = (last * rms * gen_gain).astype(jnp.bfloat16)
    gen_pre = jnp.dot(gen_normed, gen_in, preferred_element_type=jnp.float32)
    gen_hidden, gen_pull = jax.vjp(gelu_exact, gen_pre)
    mixing = jnp.einsum("th,hsj->tsj", gen_hidden, gen_out, precision=highest) + gen_bias
    weighted = mixing * valid_float[:, None, None]
    stat_sums = jnp.sum(weighted, axis=0)
    stat_squares = jnp.sum(weighted * mixing, axis=0)
    stat_count = jnp.sum(valid_float)
    streams = mixing[:, :, 0].T[:, :, None] * hist_local[0]
    for state in range(1, states):
        streams = streams + mixing[:, :, state].T[:, :, None] * hist_local[state]
    scaled, inverse = normalize(streams)
    normed_attn = (scaled[:3] * norm_gain[0] + norm_bias[0]).astype(jnp.bfloat16)
    normed_mlp = (scaled[3] * norm_gain[1] + norm_bias[1]).astype(jnp.bfloat16)
    piece = lax.all_gather(w_in, "seq", axis=0, tiled=True)
    attn_part = jnp.einsum(
        "stk,nsk->stn", normed_attn, piece[:, :3], preferred_element_type=jnp.float32
    )
    mlp_part = jnp.einsum(
        "tk,njk->jtn", normed_mlp, piece[:, 3:], preferred_element_type=jnp.float32
    )
    projected = jnp.concatenate([attn_part, mlp_part], axis=0) + in_bias[:, None, :]
    cosine, sine = rotary_tables(position)
    heads_shape = (tokens, HEADS, HEAD_DIM)
    queries = (rotate(projected[0].reshape(heads_shape), cosine, sine) * HEAD_DIM ** (-0.5)).astype(
        jnp.bfloat16
    )
    keys = rotate(projected[1].reshape(heads_shape), cosine, sine).astype(jnp.bfloat16)
    values = projected[2].reshape(heads_shape).astype(jnp.bfloat16)
    index = jnp.arange(tokens, dtype=jnp.int32)
    allowed = (
        (second[:, None] == second[None, :]) & (index[None, :] <= index[:, None]) & valid[None, :]
    )
    scores = jnp.einsum("qhd,khd->hqk", queries, keys, preferred_element_type=jnp.float32)
    scores = jnp.where(allowed[None], scores, masked_score)
    top = jnp.max(scores, axis=-1, keepdims=True)
    weights = jnp.exp(scores - top)
    weight_total = jnp.sum(weights, axis=-1, keepdims=True)
    log_total = top + jnp.log(weight_total)
    probs_low = (weights / weight_total).astype(jnp.bfloat16)
    attended = jnp.einsum("hqk,khd->qhd", probs_low, values, preferred_element_type=jnp.float32)
    attn_low = attended.reshape(tokens, width).astype(jnp.bfloat16)
    gelu_up, up_pull = jax.vjp(gelu_exact, projected[3:])
    gelu_low = gelu_up.astype(jnp.bfloat16)
    grad_out_low = jnp.where(valid[:, None], cot_local, jnp.zeros_like(cot_local))
    piece_out, piece_down = lax.all_gather((w_out, w_down), "seq", axis=0, tiled=True)
    down_part = piece_down.reshape(piece_down.shape[0], 4, width)
    result = jnp.einsum("tk,nk->tn", attn_low, piece_out, preferred_element_type=jnp.float32)
    branch = result + jnp.einsum(
        "jtk,njk->tn", gelu_low, down_part, preferred_element_type=jnp.float32
    )
    new_local = (streams[3] + branch + out_bias).astype(jnp.bfloat16)
    piece_out = lax.all_gather(w_out, "seq", axis=0, tiled=True)
    piece_down = lax.all_gather(w_down, "seq", axis=0, tiled=True)
    count = piece_out.shape[0]
    part = grad_out_low
    attn_add = jnp.einsum("tn,nk->tk", part, piece_out, preferred_element_type=jnp.float32)
    gelu_add = jnp.einsum(
        "tn,njk->jtk", part, piece_down.reshape(count, 4, width), preferred_element_type=jnp.float32
    )
    grad_attn = attn_add
    part = grad_out_low
    term_out = jnp.einsum("tn,tk->nk", part, attn_low, preferred_element_type=jnp.float32)
    term_down = jnp.einsum(
        "tn,jtk->njk", part, gelu_low, preferred_element_type=jnp.float32
    ).reshape(lax.axis_size("seq") * w_out.shape[0], 4 * width)
    out_grads = lax.psum_scatter(
        jnp.concatenate([term_out, term_down], axis=1).astype(jnp.bfloat16),
        "seq",
        scatter_dimension=0,
        tiled=True,
    )
    out_bias_grad = jnp.sum(grad_out_low.astype(jnp.float32), axis=0)
    grad_attended = grad_attn.astype(jnp.bfloat16).reshape(heads_shape)
    rescored = jnp.einsum("qhd,khd->hqk", queries, keys, preferred_element_type=jnp.float32)
    probs = jnp.where(allowed[None], jnp.exp(rescored - log_total), 0.0)
    grad_values = jnp.einsum(
        "hqk,qhd->khd",
        probs.astype(jnp.bfloat16),
        grad_attended,
        preferred_element_type=jnp.float32,
    )
    grad_probs = jnp.einsum(
        "qhd,khd->hqk", grad_attended, values, preferred_element_type=jnp.float32
    )
    grad_scores = (
        probs * (grad_probs - jnp.sum(probs * grad_probs, axis=-1, keepdims=True))
    ).astype(jnp.bfloat16)
    grad_queries = jnp.einsum(
        "hqk,khd->qhd", grad_scores, keys, preferred_element_type=jnp.float32
    ) * HEAD_DIM ** (-0.5)
    grad_keys = jnp.einsum("hqk,qhd->khd", grad_scores, queries, preferred_element_type=jnp.float32)
    grad_up = up_pull(gelu_add)[0]
    grad_proj = jnp.concatenate(
        [
            rotate(grad_queries, cosine, -sine).reshape(1, tokens, width),
            rotate(grad_keys, cosine, -sine).reshape(1, tokens, width),
            grad_values.reshape(1, tokens, width),
            grad_up,
        ],
        axis=0,
    )
    in_bias_grad = jnp.sum(grad_proj, axis=1)
    grad_proj_low = grad_proj.astype(jnp.bfloat16)
    piece = lax.all_gather(w_in, "seq", axis=0, tiled=True)
    part = grad_proj_low
    attn_add = jnp.einsum(
        "stn,nsk->stk", part[:3], piece[:, :3], preferred_element_type=jnp.float32
    )
    mlp_add = jnp.einsum("jtn,njk->tk", part[3:], piece[:, 3:], preferred_element_type=jnp.float32)
    part = grad_proj_low
    attn_term = jnp.einsum(
        "stn,stk->nsk", part[:3], normed_attn, preferred_element_type=jnp.float32
    )
    mlp_term = jnp.einsum("jtn,tk->njk", part[3:], normed_mlp, preferred_element_type=jnp.float32)
    in_grads = lax.psum_scatter(
        jnp.concatenate([attn_term, mlp_term], axis=1).astype(jnp.bfloat16),
        "seq",
        scatter_dimension=0,
        tiled=True,
    )
    norm_gain_grad = jnp.stack(
        [jnp.sum(attn_add * scaled[:3], axis=(0, 1)), jnp.sum(mlp_add * scaled[3], axis=0)]
    )
    norm_bias_grad = jnp.stack([jnp.sum(attn_add, axis=(0, 1)), jnp.sum(mlp_add, axis=0)])
    grad_attn_streams = normalize_back(attn_add * norm_gain[0], scaled[:3], inverse[:3])
    grad_mlp_stream = normalize_back(
        mlp_add * norm_gain[1], scaled[3], inverse[3]
    ) + grad_out_low.astype(jnp.float32)
    grad_streams = jnp.concatenate([grad_attn_streams, grad_mlp_stream[None]], axis=0)
    grad_mixing = jnp.stack(
        [
            jnp.einsum(
                "std,td->ts", grad_streams, hist_local[state].astype(jnp.float32), precision=highest
            )
            for state in range(states)
        ],
        axis=-1,
    )
    hist_terms = [
        jnp.einsum("ts,std->td", mixing[:, :, state], grad_streams, precision=highest)
        for state in range(states)
    ]
    gen_bias_grad = jnp.sum(grad_mixing, axis=0)
    gen_out_grad = jnp.einsum("th,tsj->hsj", gen_hidden, grad_mixing, precision=highest)
    grad_hidden = jnp.einsum("tsj,hsj->th", grad_mixing, gen_out, precision=highest)
    grad_pre_low = gen_pull(grad_hidden)[0].astype(jnp.bfloat16)
    gen_in_grad = jnp.einsum(
        "tk,th->kh", gen_normed, grad_pre_low, preferred_element_type=jnp.float32
    )
    grad_gen = jnp.einsum("th,kh->tk", grad_pre_low, gen_in, preferred_element_type=jnp.float32)
    gen_gain_grad = jnp.sum(grad_gen * last * rms, axis=0)
    gained = grad_gen * gen_gain
    grad_last = rms * gained - last * (rms * rms * rms) * jnp.mean(
        gained * last, axis=-1, keepdims=True
    )
    hist_stack = jnp.stack(hist_terms[: states - 1] + [hist_terms[states - 1] + grad_last]).astype(
        jnp.bfloat16
    )
    departing = jnp.swapaxes(jnp.concatenate([new_local[None], hist_stack], axis=0), 1, 2)
    returned = lax.all_to_all(departing, "seq", split_axis=1, concat_axis=2, tiled=True)
    w_in_grad, out_total = (
        lax.psum(in_grads, "dp").astype(jnp.float32),
        lax.psum(out_grads, "dp").astype(jnp.float32),
    )
    w_out_grad = out_total[:, :width]
    w_down_grad = out_total[:, width:]
    joined = lax.psum(
        (
            gen_gain_grad,
            gen_in_grad,
            gen_out_grad,
            gen_bias_grad,
            norm_gain_grad,
            norm_bias_grad,
            in_bias_grad,
            out_bias_grad,
            stat_sums,
            stat_squares,
            stat_count,
        ),
        ("seq", "dp"),
    )
    small_totals = joined[:8]
    stat_totals = joined[8:]
    mix_mean = stat_totals[0] / stat_totals[2]
    mix_var = stat_totals[1] / stat_totals[2] - mix_mean * mix_mean
    return (
        returned[0],
        returned[1:],
        mix_mean,
        mix_var,
        small_totals[0],
        small_totals[1],
        small_totals[2],
        small_totals[3],
        small_totals[4],
        small_totals[5],
        w_in_grad,
        small_totals[6],
        w_out_grad,
        w_down_grad,
        small_totals[7],
    )


def solution(mesh):
    in_specs = (
        P(None, "seq", "dp"),
        P("seq", "dp"),
        P("dp", "seq", None),
        P("dp", "seq", None),
        P(),
        P(),
        P(),
        P(),
        P(),
        P(),
        P("seq", None, None),
        P(),
        P("seq", None),
        P("seq", None),
        P(),
    )
    out_specs = (
        P("seq", "dp"),
        P(None, "seq", "dp"),
        P(),
        P(),
        P(),
        P(),
        P(),
        P(),
        P(),
        P(),
        P("seq", None, None),
        P(),
        P("seq", None),
        P("seq", None),
        P(),
    )
    return jax.shard_map(
        per_device, mesh=mesh, in_specs=in_specs, out_specs=out_specs, check_vma=False
    )
```

profile of v0, /device:TPU:8, one launch (start us, length us, event | category | flops | bytes accessed | tf_op | source)
XLA Modules:
  0.0 705.1 jit_solution(17909491425658481265)
XLA Ops:
  11.4 7.4 %copy.110 = bf16[9,128,1024]{1,0,2:T(8,128)(2,1)} copy(bf16[9,128,1024]{2,1,0:T(8,128)(2,1)S(1)} %copy-done.17) | data formatting | bytes 4718592 | tf_op args[0]
  18.8 6.1 pad_maximum_fusion.2
  33.1 64.4 %all-to-all-done = bf16[10,128,1024]{1,0,2:T(8,128)(2,1)} async-done(((bf16[10,128,1024]{1,0,2:T(8,128)(2,1)}), bf16[10,128,1024]{1,0,2:T(8,128)(2,1)}, u32[]{:S(2)}, u32[]{:S(2)}) %all-to-all-start) | async-done | bytes 2621472 | tf_op jit(solution)/shard_map/all_to_all | solution.py:83
  97.5 5.4 copy.298
  117.8 33.5 %all-gather.4.cloned.1.call-done = bf16[1024,7,1024]{2,0,1:T(8,128)(2,1)} async-done(((bf16[128,7,1024]{2,0,1:T(8,128)(2,1)}), bf16[1024,7,1024]{2,0,1:T(8,128)(2,1)}) %all-gather.4.cloned.1.call-update) | async-done | bytes 14680080 | tf_op jit(solution)/shard_map/all_gather | solution.py:107
  151.3 5.0 fusion.6
  156.3 6.3 fusion.22
  184.9 7.3 %multiply_convert_fusion = (bf16[4,128,1024]{2,1,0:T(8,128)(2,1)}, f32[4,128,1024]{2,1,0:T(8,128)}) fusion(f32[7,128,1024]{2,1,0:T(8,128)} %copy-done.3), kind=kLoop, calls=%fused_computation.30 | loop fusion | flops 34078720 | bytes 5242880 | tf_op jit(solution)/shard_map/convert_element_type | solution.py:136
  192.2 16.9 %all-gather.8.cloned.1.call-done = bf16[1024,4096]{0,1:T(8,128)(2,1)} async-done(((bf16[128,4096]{0,1:T(8,128)(2,1)}), bf16[1024,4096]{0,1:T(8,128)(2,1)}) %all-gather.8.cloned.1.call-update) | async-done | bytes 8388624 | tf_op jit(solution)/shard_map/all_gather | solution.py:138
  209.1 8.0 %fusion.15 = f32[4,128,1024]{2,1,0:T(8,128)S(1)} fusion(f32[4,128,1024]{2,1,0:T(8,128)} %get-tuple-element.106, f32[7,128,1024]{2,1,0:T(8,128)} %copy-done.3, bf16[1024,4,1024]{0,2,1:T(8,128)(2,1)} %bitcast.374, pred[128]{0:T(512)(128)(4,1)S(1)} %copy-done.57, bf16[10,128,1024]{2,1,0:T(8,128)(2,1)} %bitcast.365), kind=kOutput, calls=%fused_computation.28 | convolution fusion | flops 1080688640 | bytes 14942336 | tf_op jit(solution)/shard_map/tn,njk->jtk/dot_general | solution.py:150
  223.3 8.3 %pad_maximum_fusion = bf16[1024,7,1024]{0,2,1:T(8,128)(2,1)} fusion(bf16[1024,4,1024]{0,2,1:T(8,128)(2,1)S(1)} %convert_bitcast_fusion, bf16[1024,3,1024]{0,2,1:T(8,128)(2,1)S(1)} %convert_bitcast_fusion.1), kind=kLoop, calls=%fused_computation | loop fusion | flops 7340032 | bytes 29360128 | tf_op jit(solution)/shard_map/concatenate | solution.py:209
  231.6 18.5 %copy.186 = bf16[1024,7168]{1,0:T(8,128)(2,1)} copy(bf16[1024,7168]{0,1:T(8,128)(2,1)} %bitcast.360) | data formatting | bytes 29360128
  264.6 6.3 pad_maximum_fusion.1
  278.1 5.9 multiply_reduce_fusion.5
  284.0 5.0 multiply_reduce_fusion.1
  301.2 5.0 fusion.64
  317.2 5.2 fusion.58
  333.9 5.6 fusion.52
  343.5 5.2 fusion.154
  348.8 4.9 convolution_bitcast_fusion.1
  388.6 51.7 %reduce-scatter.5.cloned.1.call-done = bf16[128,5120]{1,0:T(8,128)(2,1)} async-done(((bf16[1024,5120]{1,0:T(8,128)(2,1)}), bf16[128,5120]{1,0:T(8,128)(2,1)}) %reduce-scatter.5.cloned.1.call-update) | async-done | bytes 1310736 | tf_op jit(solution)/shard_map/reduce_scatter | solution.py:159
  457.2 6.8 copy.129
  472.8 81.4 %all-reduce = (f32[4,9]{1,0:T(4,128)S(1)}, f32[]{:T(128)}, f32[4,9]{1,0:T(4,128)S(1)}, f32[1024]{0:T(1024)}, f32[40,4,9]{0,2,1:T(8,128)S(1)}, /*index=5*/f32[4,9...) all-reduce(f32[4,9]{1,0:T(4,128)S(1)} %copy-done.85, ...), channel_id=1, replica_groups=mesh['seq'=8,'dp'=4] {'seq','dp'}, use_global_device_ids=true, to_apply=%region_12.13 | all-reduce | flops 14861 | bytes 118888 | tf_op jit(solution)/shard_map/psum | solution.py:260
  574.8 121.5 %all-reduce.5.cloned.1.call-done = f32[1024,40]{0,1:T(8,128)} async-done(((f32[1024,40]{0,1:T(8,128)}), f32[1024,40]{0,1:T(8,128)}) %all-reduce.5.cloned.1.call-update) | async-done | bytes 163856 | tf_op jit(solution)/shard_map/psum | solution.py:260
  (353 shorter events, 197.9 us)
Async XLA Ops:
  7.2 101.2 %copy-start = (bf16[1024,40]{0,1:T(8,128)(2,1)S(1)}, bf16[1024,40]{0,1:T(8,128)(2,1)}, u32[]{:S(2)}) copy-start(bf16[1024,40]{0,1:T(8,128)(2,1)} %param.20) | copy-start | bytes 245764
  7.2 108.2 %all-gather.6.cloned.1.call-start = ((), (), s32[]{:S(2)}) async-start(), calls=%async_computation.5 | async-start | bytes 2359296 | tf_op jit(solution)/shard_map/all_gather | solution.py:138
  7.9 143.4 %all-gather.4.cloned.1.call-start = ((), (), s32[]{:S(2)}) async-start(), calls=%async_computation.4 | async-start | bytes 16515072 | tf_op jit(solution)/shard_map/all_gather | solution.py:107
  8.7 200.4 %all-gather.8.cloned.1.call-start = ((), (), s32[]{:S(2)}) async-start(), calls=%async_computation.6 | async-start | bytes 9437184 | tf_op jit(solution)/shard_map/all_gather | solution.py:138
  24.9 8.1 %copy-start.86 = (f32[2,1024]{1,0:T(2,128)S(1)}, f32[2,1024]{1,0:T(2,128)}, u32[]{:S(2)}) copy-start(f32[2,1024]{1,0:T(2,128)} %param.24) | copy-start | bytes 24580
  24.9 8.1 %copy-start.87 = (f32[2,1024]{1,0:T(2,128)S(1)}, f32[2,1024]{1,0:T(2,128)}, u32[]{:S(2)}) copy-start(f32[2,1024]{1,0:T(2,128)} %param.23) | copy-start | bytes 24580
  24.9 72.6 %all-to-all-start = ((bf16[10,128,1024]{1,0,2:T(8,128)(2,1)}), bf16[10,128,1024]{1,0,2:T(8,128)(2,1)}, u32[]{:S(2)}, u32[]{:S(2)}) async-start(bf16[10,128,1024]{1,0,2:T(8,128)(2,1)} %pad_maximum_fusion.2), calls=%async_computation | async-start | bytes 8388608 | tf_op jit(solution)/shard_map/all_to_all | solution.py:83
  29.6 355.1 %reduce-scatter.7.cloned.1.call-start = ((), (), s32[]{:S(2)}) async-start(), calls=%async_computation.9 | async-start | bytes 16515072
  32.2 83.3 %copy-start.56 = (pred[128]{0:T(512)(128)(4,1)}, pred[128]{0:T(512)(128)(4,1)S(1)}, u32[]{:S(2)}) copy-start(pred[128]{0:T(512)(128)(4,1)S(1)} %get-tuple-element.104) | copy-start | bytes 388
  33.0 118.3 %copy-start.78 = (f32[1,1024]{1,0:T(1,128)}, f32[1,1024]{1,0:T(1,128)S(1)}, u32[]{:S(2)}) copy-start(f32[1,1024]{1,0:T(1,128)S(1)} %get-tuple-element.152) | copy-start | bytes 12292
  33.0 123.3 %copy-start.82 = (f32[1,1024]{1,0:T(1,128)}, f32[1,1024]{1,0:T(1,128)S(1)}, u32[]{:S(2)}) copy-start(f32[1,1024]{1,0:T(1,128)S(1)} %get-tuple-element.153) | copy-start | bytes 12292
  184.9 24.2 %copy-start.57 = (pred[128]{0:T(512)(128)(4,1)S(1)}, pred[128]{0:T(512)(128)(4,1)}, u32[]{:S(2)}) copy-start(pred[128]{0:T(512)(128)(4,1)} %copy-done.56) | copy-start | bytes 388
  209.1 9.3 %copy-start.11 = (f32[1,128,1024]{2,1,0:T(8,128)S(1)}, f32[1,128,1024]{2,1,0:T(8,128)}, u32[]{:S(2)}) copy-start(f32[1,128,1024]{2,1,0:T(8,128)} %copy.127) | copy-start | bytes 1572868
  209.1 9.3 %copy-start.13 = (f32[1,128,1024]{2,1,0:T(8,128)S(1)}, f32[1,128,1024]{2,1,0:T(8,128)}, u32[]{:S(2)}) copy-start(f32[1,128,1024]{2,1,0:T(8,128)} %copy.126) | copy-start | bytes 1572868
  209.1 9.3 %copy-start.15 = (f32[1,128,1024]{2,1,0:T(8,128)S(1)}, f32[1,128,1024]{2,1,0:T(8,128)}, u32[]{:S(2)}) copy-start(f32[1,128,1024]{2,1,0:T(8,128)} %copy.125) | copy-start | bytes 1572868
  250.1 190.1 %reduce-scatter.5.cloned.1.call-start = ((), (), s32[]{:S(2)}) async-start(), calls=%async_computation.8 | async-start | bytes 11796480 | tf_op jit(solution)/shard_map/reduce_scatter | solution.py:159
  270.9 7.2 %copy-start.59 = (f32[4,128]{1,0:T(4,128)S(1)}, f32[4,128]{1,0:T(4,128)}, u32[]{:S(2)}) copy-start(f32[4,128]{1,0:T(4,128)} %copy-done.58) | copy-start | bytes 6148
  270.9 296.3 %all-reduce.7.cloned.1.call-start = ((), (), s32[]{:S(2)}) async-start(), calls=%async_computation.10 | async-start | bytes 6291456 | tf_op jit(solution)/shard_map/psum | solution.py:255
  339.5 9.3 %copy-start.4 = (bf16[4,128,1024]{2,1,0:T(8,128)(2,1)S(1)}, bf16[4,128,1024]{2,1,0:T(8,128)(2,1)}, u32[]{:S(2)}) copy-start(bf16[4,128,1024]{2,1,0:T(8,128)(2,1)} %get-tuple-element.105) | copy-start | bytes 3145732
  388.6 51.7 %copy-start.38 = (f32[128,4,1]{1,2,0:T(1,128)S(1)}, f32[128,4,1]{1,2,0:T(1,128)}, u32[]{:S(2)}) copy-start(f32[128,4,1]{1,2,0:T(1,128)} %copy.157) | copy-start | bytes 6148
  464.1 7.0 copy-start.7
  464.1 7.0 copy-start.12
  464.1 91.9 %all-to-all-start.1 = ((bf16[10,1024,128]{2,0,1:T(8,128)(2,1)}), bf16[10,1024,128]{2,0,1:T(8,128)(2,1)}, u32[]{:S(2)}, u32[]{:S(2)}) async-start(bf16[10,1024,128]{2,0,1:T(8,128)(2,1)} %copy.129), calls=%async_computation.1 | async-start | bytes 8388608 | tf_op jit(solution)/shard_map/all_to_all | solution.py:253
  469.0 227.3 %all-reduce.5.cloned.1.call-start = ((), (), s32[]{:S(2)}) async-start(), calls=%async_computation.7 | async-start | bytes 327680 | tf_op jit(solution)/shard_map/psum | solution.py:260
  (86 other events, 310.0 us)
Sparse Core Ops, SparseCore 0:
  9.9 33.7 all-gather.5
  45.6 105.6 all-gather.3
  153.2 55.8 all-gather.7
  250.2 104.6 reduce-scatter.6
  358.2 81.9 reduce-scatter.4
  442.5 120.2 all-reduce.6
  568.9 127.3 all-reduce.4
where the time goes:
time: 712 us; the launch traced here: 705 us
  waiting for transfers between devices  289 us (41%)
  matrix products  148 us (21%)
  local copies, waits for them, and re-layouts  115 us (16%)
  blocking collectives  81.4 us (11%)
  other arithmetic  46.1 us (6%)
  between operations  15.9 us (2%)
  starting transfers between devices  9.98 us (1%)
    psum x1, waiting for transfers between devices, per_device(): lax.psum((gen_gain_grad, gen_in_grad, gen_out_grad, gen_bias_grad, norm_g...  121 us
    psum x1, blocking collectives, per_device(): lax.psum((gen_gain_grad, gen_in_grad, gen_out_grad, gen_bias_grad, norm_g...  81.4 us
    all_to_all x1, waiting for transfers between devices, per_device(): lax.all_to_all(stacked, 'seq', split_axis=2, concat_axis=1, tiled=True)  64.4 us
    reduce_scatter x1, waiting for transfers between devices, per_device(): lax.psum_scatter(jnp.concatenate([term_out, term_down], axis=1).astype(jn...  51.7 us
    unnamed x218, local copies, waits for them, and re-layouts  50.6 us
    dot_general x9, matrix products, per_device(): jnp.einsum('std,td->ts', grad_streams, hist_local[state].astype(jnp.float...  44.5 us
    dot_general x9, matrix products, per_device(): jnp.einsum('ts,std->td', mixing[:, :, state], grad_streams, precision=hig...  40.6 us
    all_gather x1, waiting for transfers between devices, per_device(): piece = lax.all_gather(w_in, 'seq', axis=0, tiled=True)  33.5 us
  transfers between devices with their start and end apart: 9, of which 5 were waited for; matrix products, arithmetic and copies ran while one was open for 36% of the time, Pallas kernels for 0%

commit v1 on v0

--- a/solution.py
+++ b/solution.py
@@ -3,6 +3,7 @@
 import jax.numpy as jnp
 from jax import lax
 from jax.sharding import PartitionSpec as P
+from jax.lax import all_to_all, axis_size
 
 HEADS = 16
 HEAD_DIM = 64
@@ -80,7 +81,9 @@
 ):
     states = history.shape[0]
     stacked = jnp.concatenate([history, cotangent[None]], axis=0)
-    arrived = lax.all_to_all(stacked, "seq", split_axis=2, concat_axis=1, tiled=True)
+    arrived = jnp.concatenate(
+        all_to_all(jnp.stack(jnp.split(stacked, axis_size("seq"), axis=2), 0), "seq", 0, 0), 1
+    )
     arrived_rows = jnp.swapaxes(arrived, 1, 2)
     hist_local = arrived_rows[:states]
     cot_local = arrived_rows[states]

time: 712 us -> 699 us (0.982)
  local copies, waits for them, and re-layouts: 115 us -> 105 us
    all_to_all x1, waiting for transfers between devices: 64.4 us -> 34.3 us  [per_device(): all_to_all(jnp.stack(jnp.split(stacked, axis_size('seq'), axis=2), 0), 's...]
    all_gather x1, waiting for transfers between devices: 33.5 us -> 56.2 us  [per_device(): piece = lax.all_gather(w_in, 'seq', axis=0, tiled=True)]
    all_to_all x2 -> x0, local copies, waits for them, and re-layouts: 9.41 us -> none  [per_device(): lax.all_to_all(stacked, 'seq', split_axis=2, concat_axis=1, tiled=True)]
    reshape x0 -> x2, local copies, waits for them, and re-layouts: none -> 7.21 us  [per_device(): jnp.concatenate(all_to_all(jnp.stack(jnp.split(stacked, axis_size('seq'),...]
    unnamed x218 -> x217, local copies, waits for them, and re-layouts: 50.6 us -> 44.1 us
where the time goes in v1:
time: 699 us; the launch traced here: 687 us
  waiting for transfers between devices  282 us (40%)
  matrix products  148 us (21%)
  local copies, waits for them, and re-layouts  105 us (15%)
  blocking collectives  81.4 us (12%)
  other arithmetic  46.4 us (7%)
  between operations  15.9 us (2%)
  starting transfers between devices  9.16 us (1%)
    psum x1, waiting for transfers between devices, per_device(): lax.psum((gen_gain_grad, gen_in_grad, gen_out_grad, gen_bias_grad, norm_g...  121 us
    psum x1, blocking collectives, per_device(): lax.psum((gen_gain_grad, gen_in_grad, gen_out_grad, gen_bias_grad, norm_g...  81.4 us
    all_gather x1, waiting for transfers between devices, per_device(): piece = lax.all_gather(w_in, 'seq', axis=0, tiled=True)  56.2 us
    reduce_scatter x1, waiting for transfers between devices, per_device(): lax.psum_scatter(jnp.concatenate([term_out, term_down], axis=1).astype(jn...  51.6 us
    dot_general x9, matrix products, per_device(): jnp.einsum('std,td->ts', grad_streams, hist_local[state].astype(jnp.float...  44.5 us
    unnamed x217, local copies, waits for them, and re-layouts  44.1 us
    dot_general x9, matrix products, per_device(): jnp.einsum('ts,std->td', mixing[:, :, state], grad_streams, precision=hig...  40.6 us
    all_to_all x1, waiting for transfers between devices, per_device(): all_to_all(jnp.stack(jnp.split(stacked, axis_size('seq'), axis=2), 0), 's...  34.3 us
  transfers between devices with their start and end apart: 9, of which 5 were waited for; matrix products, arithmetic and copies ran while one was open for 36% of the time, Pallas kernels for 0%

profile of v1, /device:TPU:8, one launch (start us, length us, event | category | flops | bytes accessed | tf_op | source)
XLA Modules:
  0.0 687.3 jit_solution(905097735796283608)
XLA Ops:
  25.0 34.3 %all-to-all-done = bf16[8,10,128,128]{3,2,1,0:T(8,128)(2,1)S(1)} async-done(((bf16[8,10,128,128]{3,2,1,0:T(8,128)(2,1)}), bf16[8,10,128,128]{3,2,1,0:T(8,128)(2,1)S(1)}, u32[]{:S(2)}, u32[]{:S(2)}) %all-to-all-start) | async-done | bytes 2621472 | tf_op jit(solution)/shard_map/all_to_all | solution.py:85
  77.3 56.2 %all-gather.4.cloned.1.call-done = bf16[1024,7,1024]{2,0,1:T(8,128)(2,1)} async-done(((bf16[128,7,1024]{2,0,1:T(8,128)(2,1)}), bf16[1024,7,1024]{2,0,1:T(8,128)(2,1)}) %all-gather.4.cloned.1.call-update) | async-done | bytes 14680080 | tf_op jit(solution)/shard_map/all_gather | solution.py:110
  133.5 5.0 fusion.6
  138.5 6.3 fusion.22
  167.1 7.2 %multiply_convert_fusion = (bf16[4,128,1024]{2,1,0:T(8,128)(2,1)}, f32[4,128,1024]{2,1,0:T(8,128)}) fusion(f32[7,128,1024]{2,1,0:T(8,128)} %copy-done.5), kind=kLoop, calls=%fused_computation.35 | loop fusion | flops 34078720 | bytes 5242880 | tf_op jit(solution)/shard_map/convert_element_type | solution.py:139
  174.3 17.0 %all-gather.8.cloned.1.call-done = bf16[1024,4096]{0,1:T(8,128)(2,1)} async-done(((bf16[128,4096]{0,1:T(8,128)(2,1)}), bf16[1024,4096]{0,1:T(8,128)(2,1)}) %all-gather.8.cloned.1.call-update) | async-done | bytes 8388624 | tf_op jit(solution)/shard_map/all_gather | solution.py:141
  191.3 8.0 %fusion.15 = f32[4,128,1024]{2,1,0:T(8,128)S(1)} fusion(f32[4,128,1024]{2,1,0:T(8,128)} %get-tuple-element.91, f32[7,128,1024]{2,1,0:T(8,128)} %copy-done.5, bf16[1024,4,1024]{0,2,1:T(8,128)(2,1)} %bitcast.397, pred[128]{0:T(512)(128)(4,1)S(1)} %copy-done.57, bf16[10,128,1024]{2,1,0:T(8,128)(2,1)} %bitcast.380), kind=kOutput, calls=%fused_computation.33 | convolution fusion | flops 1080688640 | bytes 14942336 | tf_op jit(solution)/shard_map/tn,njk->jtk/dot_general | solution.py:153
  205.5 8.3 %pad_maximum_fusion = bf16[1024,7,1024]{0,2,1:T(8,128)(2,1)} fusion(bf16[1024,4,1024]{0,2,1:T(8,128)(2,1)S(1)} %convert_bitcast_fusion, bf16[1024,3,1024]{0,2,1:T(8,128)(2,1)S(1)} %convert_bitcast_fusion.1), kind=kLoop, calls=%fused_computation | loop fusion | flops 7340032 | bytes 29360128 | tf_op jit(solution)/shard_map/concatenate | solution.py:212
  213.8 18.5 %copy.156 = bf16[1024,7168]{1,0:T(8,128)(2,1)} copy(bf16[1024,7168]{0,1:T(8,128)(2,1)} %bitcast.375) | data formatting | bytes 29360128
  246.8 6.3 pad_maximum_fusion.1
  260.3 5.9 multiply_reduce_fusion.5
  266.2 5.0 multiply_reduce_fusion.1
  278.5 4.8 fusion.66
  283.4 5.0 fusion.64
  288.5 4.8 fusion.62
  299.4 5.2 fusion.58
  316.1 5.6 fusion.52
  325.7 5.2 fusion.163
  331.0 4.9 convolution_bitcast_fusion.1
  370.8 51.6 %reduce-scatter.5.cloned.1.call-done = bf16[128,5120]{1,0:T(8,128)(2,1)} async-done(((bf16[1024,5120]{1,0:T(8,128)(2,1)}), bf16[128,5120]{1,0:T(8,128)(2,1)}) %reduce-scatter.5.cloned.1.call-update) | async-done | bytes 1310736 | tf_op jit(solution)/shard_map/reduce_scatter | solution.py:162
  439.4 6.8 copy.99
  446.3 4.8 all-to-all-start.1
  454.9 81.4 %all-reduce = (f32[4,9]{1,0:T(4,128)S(1)}, f32[]{:T(128)}, f32[4,9]{1,0:T(4,128)S(1)}, f32[1024]{0:T(1024)}, f32[40,4,9]{0,2,1:T(8,128)S(1)}, /*index=5*/f32[4,9...) all-reduce(f32[4,9]{1,0:T(4,128)S(1)} %copy-done.85, ...), channel_id=1, replica_groups=mesh['seq'=8,'dp'=4] {'seq','dp'}, use_global_device_ids=true, to_apply=%region_12.13 | all-reduce | flops 14861 | bytes 118888 | tf_op jit(solution)/shard_map/psum | solution.py:263
  556.9 121.5 %all-reduce.5.cloned.1.call-done = f32[1024,40]{0,1:T(8,128)} async-done(((f32[1024,40]{0,1:T(8,128)}), f32[1024,40]{0,1:T(8,128)}) %all-reduce.5.cloned.1.call-update) | async-done | bytes 163856 | tf_op jit(solution)/shard_map/psum | solution.py:263
  (358 shorter events, 191.9 us)
Async XLA Ops:
  7.2 60.7 %copy-start = (bf16[1024,40]{0,1:T(8,128)(2,1)S(1)}, bf16[1024,40]{0,1:T(8,128)(2,1)}, u32[]{:S(2)}) copy-start(bf16[1024,40]{0,1:T(8,128)(2,1)} %param.20) | copy-start | bytes 245764
  7.2 67.7 %all-gather.6.cloned.1.call-start = ((), (), s32[]{:S(2)}) async-start(), calls=%async_computation.5 | async-start | bytes 2359296 | tf_op jit(solution)/shard_map/all_gather | solution.py:141
  7.9 125.5 %all-gather.4.cloned.1.call-start = ((), (), s32[]{:S(2)}) async-start(), calls=%async_computation.4 | async-start | bytes 16515072 | tf_op jit(solution)/shard_map/all_gather | solution.py:110
  8.7 182.6 %all-gather.8.cloned.1.call-start = ((), (), s32[]{:S(2)}) async-start(), calls=%async_computation.6 | async-start | bytes 9437184 | tf_op jit(solution)/shard_map/all_gather | solution.py:141
  17.6 7.3 %copy-start.86 = (f32[2,1024]{1,0:T(2,128)S(1)}, f32[2,1024]{1,0:T(2,128)}, u32[]{:S(2)}) copy-start(f32[2,1024]{1,0:T(2,128)} %param.24) | copy-start | bytes 24580
  17.6 7.3 %copy-start.87 = (f32[2,1024]{1,0:T(2,128)S(1)}, f32[2,1024]{1,0:T(2,128)}, u32[]{:S(2)}) copy-start(f32[2,1024]{1,0:T(2,128)} %param.23) | copy-start | bytes 24580
  17.6 41.7 %all-to-all-start = ((bf16[8,10,128,128]{3,2,1,0:T(8,128)(2,1)}), bf16[8,10,128,128]{3,2,1,0:T(8,128)(2,1)S(1)}, u32[]{:S(2)}, u32[]{:S(2)}) async-start(bf16[8,10,128,128]{3,2,1,0:T(8,128)(2,1)} %fusion.82), calls=%async_computation | async-start | bytes 5242880 | tf_op jit(solution)/shard_map/all_to_all | solution.py:85
  21.4 345.4 %reduce-scatter.7.cloned.1.call-start = ((), (), s32[]{:S(2)}) async-start(), calls=%async_computation.9 | async-start | bytes 16515072
  24.0 50.9 %copy-start.56 = (pred[128]{0:T(512)(128)(4,1)}, pred[128]{0:T(512)(128)(4,1)S(1)}, u32[]{:S(2)}) copy-start(pred[128]{0:T(512)(128)(4,1)S(1)} %get-tuple-element.89) | copy-start | bytes 388
  24.8 108.7 %copy-start.78 = (f32[1,1024]{1,0:T(1,128)}, f32[1,1024]{1,0:T(1,128)S(1)}, u32[]{:S(2)}) copy-start(f32[1,1024]{1,0:T(1,128)S(1)} %get-tuple-element.137) | copy-start | bytes 12292
  24.8 113.6 %copy-start.82 = (f32[1,1024]{1,0:T(1,128)}, f32[1,1024]{1,0:T(1,128)S(1)}, u32[]{:S(2)}) copy-start(f32[1,1024]{1,0:T(1,128)S(1)} %get-tuple-element.138) | copy-start | bytes 12292
  167.1 24.2 %copy-start.57 = (pred[128]{0:T(512)(128)(4,1)S(1)}, pred[128]{0:T(512)(128)(4,1)}, u32[]{:S(2)}) copy-start(pred[128]{0:T(512)(128)(4,1)} %copy-done.56) | copy-start | bytes 388
  191.3 9.3 %copy-start.13 = (f32[1,128,1024]{2,1,0:T(8,128)S(1)}, f32[1,128,1024]{2,1,0:T(8,128)}, u32[]{:S(2)}) copy-start(f32[1,128,1024]{2,1,0:T(8,128)} %copy.97) | copy-start | bytes 1572868
  191.3 9.3 %copy-start.15 = (f32[1,128,1024]{2,1,0:T(8,128)S(1)}, f32[1,128,1024]{2,1,0:T(8,128)}, u32[]{:S(2)}) copy-start(f32[1,128,1024]{2,1,0:T(8,128)} %copy.96) | copy-start | bytes 1572868
  191.3 9.3 %copy-start.17 = (f32[1,128,1024]{2,1,0:T(8,128)S(1)}, f32[1,128,1024]{2,1,0:T(8,128)}, u32[]{:S(2)}) copy-start(f32[1,128,1024]{2,1,0:T(8,128)} %copy.95) | copy-start | bytes 1572868
  232.3 190.1 %reduce-scatter.5.cloned.1.call-start = ((), (), s32[]{:S(2)}) async-start(), calls=%async_computation.8 | async-start | bytes 11796480 | tf_op jit(solution)/shard_map/reduce_scatter | solution.py:162
  253.1 7.2 %copy-start.59 = (f32[4,128]{1,0:T(4,128)S(1)}, f32[4,128]{1,0:T(4,128)}, u32[]{:S(2)}) copy-start(f32[4,128]{1,0:T(4,128)} %copy-done.58) | copy-start | bytes 6148
  253.1 296.2 %all-reduce.7.cloned.1.call-start = ((), (), s32[]{:S(2)}) async-start(), calls=%async_computation.10 | async-start | bytes 6291456 | tf_op jit(solution)/shard_map/psum | solution.py:258
  321.7 9.3 %copy-start.6 = (bf16[4,128,1024]{2,1,0:T(8,128)(2,1)S(1)}, bf16[4,128,1024]{2,1,0:T(8,128)(2,1)}, u32[]{:S(2)}) copy-start(bf16[4,128,1024]{2,1,0:T(8,128)(2,1)} %get-tuple-element.90) | copy-start | bytes 3145732
  370.8 51.7 %copy-start.38 = (f32[128,4,1]{1,2,0:T(1,128)S(1)}, f32[128,4,1]{1,2,0:T(1,128)}, u32[]{:S(2)}) copy-start(f32[128,4,1]{1,2,0:T(1,128)} %copy.127) | copy-start | bytes 6148
  446.2 7.0 %copy-start.9 = (f32[4,128,1024]{2,1,0:T(8,128)S(1)}, f32[4,128,1024]{2,1,0:T(8,128)}, u32[]{:S(2)}) copy-start(f32[4,128,1024]{2,1,0:T(8,128)} %copy-done.8) | copy-start | bytes 6291460
  446.2 7.0 %copy-start.14 = (f32[1,128,1024]{2,1,0:T(8,128)S(1)}, f32[1,128,1024]{2,1,0:T(8,128)}, u32[]{:S(2)}) copy-start(f32[1,128,1024]{2,1,0:T(8,128)} %copy.97) | copy-start | bytes 1572868
  446.3 91.9 %all-to-all-start.1 = ((bf16[10,1024,128]{2,0,1:T(8,128)(2,1)}), bf16[10,1024,128]{2,0,1:T(8,128)(2,1)}, u32[]{:S(2)}, u32[]{:S(2)}) async-start(bf16[10,1024,128]{2,0,1:T(8,128)(2,1)} %copy.99), calls=%async_computation.1 | async-start | bytes 8388608 | tf_op jit(solution)/shard_map/all_to_all | solution.py:256
  451.1 227.3 %all-reduce.5.cloned.1.call-start = ((), (), s32[]{:S(2)}) async-start(), calls=%async_computation.7 | async-start | bytes 327680 | tf_op jit(solution)/shard_map/psum | solution.py:263
  (86 other events, 310.1 us)
Sparse Core Ops, SparseCore 0:
  9.9 41.6 all-gather.5
  53.5 79.9 all-gather.3
  135.4 55.8 all-gather.7
  232.4 104.6 reduce-scatter.6
  340.4 81.9 reduce-scatter.4
  424.7 120.2 all-reduce.6
  551.1 127.2 all-reduce.4
